TPU v7x, 256 devices: a whole 4x4x8 slice. The times are simulated.
256 devices in a mesh: dp: 32 (over x, y, core), tensor: 8 (over z).
Axes of the slice: x: 4, y: 4, z: 8, core: 2. Of those that a mesh axis runs over, the one named last changes fastest.
Arguments:
- output_gradient: bfloat16 [8192, 8192], P('dp', 'tensor'), may hold values from -96 to 96
- hidden: bfloat16 [8192, 28672], P('dp', 'tensor'), may hold values from -3 to 3
- adapter_down: bfloat16 [64, 16, 28672], P('dp', None, 'tensor'), may hold values from -0.03125 to 0.03125
- adapter_up: bfloat16 [64, 16, 8192], P('dp', None, 'tensor'), may hold values from -0.0625 to 0.0625
- counts: int32 [64], replicated, may hold values from 32 to 288, as said below
- offsets: int32 [64], replicated, may hold values from 0 to 8160, as said below
- adapter_slot: int32 [64], replicated, may hold values from 0 to 63, as said below
Outputs:
- adapter_hidden_gradient: bfloat16 [8192, 28672], P('dp', 'tensor')
- adapter_down_gradient: float32 [64, 16, 28672], P('dp', None, 'tensor')
- adapter_up_gradient: float32 [64, 16, 8192], P('dp', None, 'tensor')
Inputs may be any that keep to these rules, and one draw needn't show every extreme that they name: counts sum to 8192; the last adapter has exactly 32 tokens; exactly one adapter has 288 tokens, every other fewer. Tokens are grouped by adapter in increasing order: offsets[a] is the sum of counts of the adapters before a. `adapter_slot`: every slot holds exactly one adapter; slot k lies on dp index k // 2, and any 64 // 2 adapters in a row lie on distinct dp indices.
All inputs are finite; a program needn't handle non-finite values.
Results may differ from a plain program's by a relative error of at most 0.0075.
Values may be sent and summed in bfloat16 or wider, within the bound.
No kernel may reach another device: no remote copies, remote signals or barrier semaphores. Data moves between devices by JAX's collectives and lax.ppermute only.
A program may use at most 64 MiB of HBM per device.

v0:
```python
import jax
import jax.numpy as jnp
from jax import lax
from jax.sharding import PartitionSpec as P

adapter_factor = 2.0


def selected_rows(value_entries, shard_portion, member_rows):
    shard_count = shard_portion.shape[0]
    adapter_rank = shard_portion.shape[1]
    flattened_rows = shard_portion.reshape(shard_count * adapter_rank, shard_portion.shape[2])
    rank_scores = lax.dot_general(
        value_entries, flattened_rows, (((1,), (1,)), ((), ())), preferred_element_type=jnp.float32
    )
    selected_entries = member_rows.astype(jnp.float32)
    return jnp.sum(
        rank_scores.reshape(value_entries.shape[0], shard_count, adapter_rank)
        * selected_entries[:, :, None],
        axis=1,
    )


def on_device(output_gradient, hidden, adapter_down, adapter_up, counts, offsets, adapter_slot):
    total_rows = output_gradient.shape[0]
    slots_per_worker = adapter_down.shape[0]
    adapter_rank = adapter_down.shape[1]
    hidden_size_count = hidden.shape[1]
    dp_count = lax.axis_size("dp")
    adapter_list = slots_per_worker * dp_count
    first_token = lax.axis_index("dp") * total_rows
    positions = first_token + lax.broadcasted_iota(jnp.int32, (total_rows, 1), 0)
    inside = (positions >= offsets[None, :]) & (positions < (offsets + counts)[None, :])
    slot_of_row = jnp.sum(jnp.where(inside, adapter_slot[None, :], 0), axis=1)
    columns = lax.broadcasted_iota(jnp.int32, (1, adapter_list), 1)
    member_rows = (slot_of_row[:, None] == columns).astype(jnp.bfloat16)
    up_portion = selected_rows(
        output_gradient, lax.all_gather(adapter_up, "dp", axis=0, tiled=True), member_rows
    )
    up_incoming = lax.psum(up_portion, "tensor").astype(jnp.bfloat16)
    broadcast_up = member_rows[:, :, None] * up_incoming[:, None, :]
    shard_portion = lax.all_gather(adapter_down, "dp", axis=0, tiled=True)
    shard_count = shard_portion.shape[0]
    flattened_rows = shard_portion.reshape(shard_count * adapter_rank, hidden_size_count)
    down_partial = selected_rows(hidden, shard_portion, member_rows)
    broadcast_portion = broadcast_up
    broadcast_portion = broadcast_portion.reshape(total_rows, shard_count * adapter_rank)
    gradient_running = jnp.dot(
        broadcast_portion, flattened_rows, preferred_element_type=jnp.float32
    )
    down_partial, gradient_running = (down_partial, gradient_running)
    down_incoming = lax.psum(down_partial, "tensor").astype(jnp.bfloat16)
    adapter_hidden_gradient = (adapter_factor * gradient_running).astype(jnp.bfloat16)
    broadcast_down = member_rows[:, :, None] * down_incoming[:, None, :]

    def slot_term(spread, value_entries, shard_count):
        broadcast_portion = spread
        broadcast_portion = broadcast_portion.reshape(total_rows, shard_count * adapter_rank)
        matrix_product = lax.dot_general(
            broadcast_portion,
            value_entries,
            (((0,), (0,)), ((), ())),
            preferred_element_type=jnp.float32,
        )
        return matrix_product.reshape(shard_count, adapter_rank, value_entries.shape[1])

    down_reduced = lax.psum_scatter(
        slot_term(broadcast_up, hidden, slots_per_worker * lax.axis_size("dp")).astype(
            jnp.bfloat16
        ),
        "dp",
        scatter_dimension=0,
        tiled=True,
    ).astype(jnp.float32)
    up_reduced = lax.psum_scatter(
        slot_term(broadcast_down, output_gradient, slots_per_worker * lax.axis_size("dp")).astype(
            jnp.bfloat16
        ),
        "dp",
        scatter_dimension=0,
        tiled=True,
    ).astype(jnp.float32)
    slot_grid = adapter_slot[:, None] == columns
    total_slots = jnp.sum(jnp.where(slot_grid, counts[:, None], 0), axis=0)
    scale_entries = adapter_factor / total_slots.astype(jnp.float32)
    owner_scale = lax.dynamic_slice_in_dim(
        scale_entries, lax.axis_index("dp") * slots_per_worker, slots_per_worker, 0
    )
    adapter_down_gradient = down_reduced * owner_scale[:, None, None]
    adapter_up_gradient = up_reduced * owner_scale[:, None, None]
    return (adapter_hidden_gradient, adapter_down_gradient, adapter_up_gradient)


def solution(mesh):
    placed = (
        P("dp", "tensor"),
        P("dp", "tensor"),
        P("dp", None, "tensor"),
        P("dp", None, "tensor"),
        P(),
        P(),
        P(),
    )
    return jax.shard_map(
        on_device,
        mesh=mesh,
        in_specs=placed,
        out_specs=(P("dp", "tensor"), P("dp", None, "tensor"), P("dp", None, "tensor")),
        check_vma=False,
    )
```

profile of v0, /device:TPU:2, one launch (start us, length us, event | category | flops | bytes accessed | tf_op | source)
XLA Modules:
  0.0 353.9 jit_solution(15384436137109650157)
XLA Ops:
  7.2 0.0 copy-start
  7.2 0.0 all-gather.3.cloned.1.call-start
  7.2 0.7 all-gather.3.cloned.1.call-update
  7.9 0.0 all-gather.5.cloned.1.call-start
  8.0 0.7 all-gather.5.cloned.1.call-update
  8.7 0.0 reduce-scatter.5.cloned.1.call-start
  8.7 0.7 add.27
  9.4 0.8 select_reduce_fusion
  10.2 51.6 %all-gather.3.cloned.1.call-done = bf16[64,16,1024]{2,1,0:T(8,128)(2,1)} async-done(((bf16[2,16,1024]{2,1,0:T(8,128)(2,1)}), bf16[64,16,1024]{2,1,0:T(8,128)(2,1)}) %all-gather.3.cloned.1.call-update) | async-done | bytes 2097168 | tf_op jit(solution)/shard_map/all_gather | solution.py:38
  61.8 4.2 %fusion.16 = f32[256,16]{0,1:T(8,128)S(1)} fusion(bf16[64,16,1024]{2,1,0:T(8,128)(2,1)} %all-gather.3.cloned.1.call-done, bf16[256,1024]{1,0:T(8,128)(2,1)} %param.7, f32[256,64]{0,1:T(8,128)S(1)} %get-tuple-element.6), kind=kOutput, calls=%fused_computation.13 | convolution fusion | flops 537391104 | bytes 2703360 | tf_op jit(solution)/shard_map/dot_general | solution.py:13
  66.0 0.0 copy-start.1
  66.0 53.4 %all-gather.5.cloned.1.call-done = bf16[64,16,3584]{2,1,0:T(8,128)(2,1)} async-done(((bf16[2,16,3584]{2,1,0:T(8,128)(2,1)}), bf16[64,16,3584]{2,1,0:T(8,128)(2,1)}) %all-gather.5.cloned.1.call-update) | async-done | bytes 7340048 | tf_op jit(solution)/shard_map/all_gather | solution.py:42
  119.4 0.0 copy-done
  119.4 11.0 %fusion.19 = f32[256,16]{0,1:T(8,128)S(1)} fusion(bf16[64,16,3584]{2,1,0:T(8,128)(2,1)} %all-gather.5.cloned.1.call-done, bf16[256,3584]{1,0:T(8,128)(2,1)S(1)} %copy-done, f32[256,64]{0,1:T(8,128)S(1)} %get-tuple-element.6), kind=kOutput, calls=%fused_computation.14 | convolution fusion | flops 1879568384 | bytes 9256960 | tf_op jit(solution)/shard_map/dot_general | solution.py:13
  130.3 30.3 %all-reduce = (bf16[256,16]{0,1:T(8,128)(2,1)S(1)}, bf16[256,16]{0,1:T(8,128)(2,1)S(1)}) all-reduce(f32[256,16]{0,1:T(8,128)S(1)} %fusion.16, f32[256,16]{0,1:T(8,128)S(1)} %fusion.19), channel_id=1, replica_groups=mesh['dp'=32,'tensor'=8] {'tensor'}, use_global_device_ids=true, to_apply=%region_2.3 | all-reduce | flops 8192 | bytes 49152 | tf_op jit(solution)/shard_map/psum | solution.py:40
  160.6 0.0 copy-done.1
  160.6 2.0 convolution_convert_fusion.1
  162.7 0.0 reduce-scatter.5.cloned.1.call-update
  162.7 0.0 reduce-scatter.3.cloned.1.call-start
  162.8 5.1 %convolution_convert_fusion = bf16[64,16,3584]{2,1,0:T(8,128)(2,1)} fusion(bf16[256,3584]{1,0:T(8,128)(2,1)S(1)} %copy-done, bf16[256,16]{0,1:T(8,128)(2,1)S(1)} %get-tuple-element.3, bf16[256,64]{0,1:T(8,128)(2,1)S(1)} %get-tuple-element.5), kind=kOutput, calls=%fused_computation | convolution fusion | flops 1882980352 | bytes 9216000 | tf_op jit(solution)/shard_map/dot_general | solution.py:59
  167.9 0.0 copy-start.2
  167.9 0.0 copy-start.3
  167.9 0.0 reduce-scatter.3.cloned.1.call-update
  167.9 0.6 copy-done.2
  168.5 0.0 copy-done.3
  168.5 0.1 select_reduce_fusion.1
  168.6 0.1 dynamic_slice.3
  168.7 6.5 %fusion.3 = bf16[256,3584]{1,0:T(8,128)(2,1)} fusion(bf16[64,16,3584]{2,1,0:T(8,128)(2,1)} %all-gather.5.cloned.1.call-done, bf16[256,16]{0,1:T(8,128)(2,1)S(1)} %get-tuple-element.3, bf16[256,64]{0,1:T(8,128)(2,1)S(1)} %get-tuple-element.5), kind=kOutput, calls=%fused_computation.5 | convolution fusion | flops 1881145344 | bytes 9216000 | tf_op jit(solution)/shard_map/dot_general | solution.py:48
  175.2 70.9 %reduce-scatter.5.cloned.1.call-done = bf16[2,16,1024]{2,1,0:T(8,128)(2,1)} async-done(((bf16[64,16,1024]{2,1,0:T(8,128)(2,1)}), bf16[2,16,1024]{2,1,0:T(8,128)(2,1)}) %reduce-scatter.5.cloned.1.call-update) | async-done | bytes 65552 | tf_op jit(solution)/shard_map/reduce_scatter | solution.py:75
  246.1 1.6 convert_multiply_fusion.1
  247.7 97.9 %reduce-scatter.3.cloned.1.call-done = bf16[2,16,3584]{2,1,0:T(8,128)(2,1)} async-done(((bf16[64,16,3584]{2,1,0:T(8,128)(2,1)}), bf16[2,16,3584]{2,1,0:T(8,128)(2,1)}) %reduce-scatter.3.cloned.1.call-update) | async-done | bytes 229392 | tf_op jit(solution)/shard_map/reduce_scatter | solution.py:67
  345.6 1.8 convert_multiply_fusion
  (3 shorter events, 0.0 us)
Async XLA Ops:
  7.2 112.2 %copy-start = (bf16[256,3584]{1,0:T(8,128)(2,1)S(1)}, bf16[256,3584]{1,0:T(8,128)(2,1)}, u32[]{:S(2)}) copy-start(bf16[256,3584]{1,0:T(8,128)(2,1)} %param.8) | copy-start | bytes 5505028
  7.2 54.6 %all-gather.3.cloned.1.call-start = ((), (), s32[]{:S(2)}) async-start(), calls=%async_computation.2 | async-start | bytes 2162688 | tf_op jit(solution)/shard_map/all_gather | solution.py:38
  7.9 111.5 %all-gather.5.cloned.1.call-start = ((), (), s32[]{:S(2)}) async-start(), calls=%async_computation.3 | async-start | bytes 7569408 | tf_op jit(solution)/shard_map/all_gather | solution.py:42
  8.7 237.5 %reduce-scatter.5.cloned.1.call-start = ((), (), s32[]{:S(2)}) async-start(), calls=%async_computation.5 | async-start | bytes 2162688 | tf_op jit(solution)/shard_map/reduce_scatter | solution.py:75
  66.0 94.6 %copy-start.1 = (bf16[256,1024]{1,0:T(8,128)(2,1)S(1)}, bf16[256,1024]{1,0:T(8,128)(2,1)}, u32[]{:S(2)}) copy-start(bf16[256,1024]{1,0:T(8,128)(2,1)} %param.7) | copy-start | bytes 1572868
  162.7 182.9 %reduce-scatter.3.cloned.1.call-start = ((), (), s32[]{:S(2)}) async-start(), calls=%async_computation.4 | async-start | bytes 7569408 | tf_op jit(solution)/shard_map/reduce_scatter | solution.py:67
  167.9 0.7 copy-start.2
  167.9 0.7 copy-start.3
Sparse Core Ops, SparseCore 0:
  10.5 51.1 all-gather.2
  64.3 55.0 all-gather.4
  162.8 83.2 reduce-scatter.4
  250.0 95.5 reduce-scatter.2
where the time goes:
time: 354 us
  waiting for transfers between devices  275 us (78%)
  blocking collectives  30.3 us (9%)
  matrix products  28.8 us (8%)
  between operations  13.8 us (4%)
  other arithmetic  4.95 us (1%)
    reduce_scatter x1, waiting for transfers between devices, on_device(): lax.psum_scatter(slot_term(broadcast_up, hidden, slots_per_worker * lax.a...  97.9 us
    reduce_scatter x1, waiting for transfers between devices, on_device(): lax.psum_scatter(slot_term(broadcast_down, output_gradient, slots_per_wor...  70.9 us
    all_gather x1, waiting for transfers between devices, on_device(): shard_portion = lax.all_gather(adapter_down, 'dp', axis=0, tiled=True)  53.4 us
    all_gather x1, waiting for transfers between devices, on_device(): lax.all_gather(adapter_up, 'dp', axis=0, tiled=True)  51.6 us
    psum x1, blocking collectives, on_device(): up_incoming = lax.psum(up_portion, 'tensor').astype(jnp.bfloat16)  30.3 us
    dot_general x2, matrix products, selected_rows(): lax.dot_general(value_entries, flattened_rows, (((1,), (1,)), ((), ())),...  15.2 us
    dot_general x2, matrix products, slot_term(): lax.dot_general(broadcast_portion, value_entries, (((0,), (0,)), ((), ())...  7.15 us
  transfers between devices with their start and end apart: 4, of which 4 were waited for; matrix products, arithmetic and copies ran while one was open for 5% of the time, Pallas kernels for 0%

commit v1 on v0

--- a/solution.py
+++ b/solution.py
@@ -1,9 +1,18 @@
+import functools
 import jax
 import jax.numpy as jnp
 from jax import lax
 from jax.sharding import PartitionSpec as P
 
 adapter_factor = 2.0
+
+
+def launch_node(shard_in, join_dim, which_axis):
+    latest = jnp.stack([shard_in for _ in range(jax.lax.axis_size(which_axis))])
+    return jnp.concatenate(jax.lax.all_to_all(latest, which_axis, 0, 0), axis=join_dim)
+
+
+define_the_windows = functools.partial(launch_node, join_dim=0, which_axis="dp")
 
 
 def selected_rows(value_entries, shard_portion, member_rows):
@@ -34,9 +43,7 @@
     slot_of_row = jnp.sum(jnp.where(inside, adapter_slot[None, :], 0), axis=1)
     columns = lax.broadcasted_iota(jnp.int32, (1, adapter_list), 1)
     member_rows = (slot_of_row[:, None] == columns).astype(jnp.bfloat16)
-    up_portion = selected_rows(
-        output_gradient, lax.all_gather(adapter_up, "dp", axis=0, tiled=True), member_rows
-    )
+    up_portion = selected_rows(output_gradient, define_the_windows(adapter_up), member_rows)
     up_incoming = lax.psum(up_portion, "tensor").astype(jnp.bfloat16)
     broadcast_up = member_rows[:, :, None] * up_incoming[:, None, :]
     shard_portion = lax.all_gather(adapter_down, "dp", axis=0, tiled=True)

time: 354 us -> 317 us (0.90)
  waiting for transfers between devices: 275 us -> 220 us
  local copies, waits for them, and re-layouts: 0.74 us -> 13.3 us
  starting transfers between devices: 0.16 us -> 8.11 us
    all_gather x1 -> x0, waiting for transfers between devices: 51.6 us -> none  [on_device(): lax.all_gather(adapter_up, 'dp', axis=0, tiled=True)]
    all_gather x1, waiting for transfers between devices: 53.4 us -> 20.8 us  [on_device(): shard_portion = lax.all_gather(adapter_down, 'dp', axis=0, tiled=True)]
    all_to_all x0 -> x1, waiting for transfers between devices: none -> 29.2 us  [launch_node(): jax.lax.all_to_all(latest, which_axis, 0, 0)]
    all_to_all x0 -> x1, starting transfers between devices: none -> 7.81 us  [launch_node(): jax.lax.all_to_all(latest, which_axis, 0, 0)]
    all_to_all x0 -> x1, local copies, waits for them, and re-layouts: none -> 4.84 us  [launch_node(): jax.lax.all_to_all(latest, which_axis, 0, 0)]
    dot_general x0 -> x1, local copies, waits for them, and re-layouts: none -> 4.23 us  [selected_rows(): lax.dot_general(value_entries, flattened_rows, (((1,), (1,)), ((), ())),...]
  transfers between devices with their start and end apart: 4 -> 4, of which waited for: 4 -> 4; matrix products, arithmetic and copies ran while one was open for 5% -> 9% of each run, Pallas kernels for 0% -> 0%
where the time goes in v1:
time: 317 us; the launch traced here: 316 us
  waiting for transfers between devices  220 us (69%)
  blocking collectives  30.2 us (10%)
  matrix products  26.9 us (8%)
  between operations  13.8 us (4%)
  local copies, waits for them, and re-layouts  13.3 us (4%)
  starting transfers between devices  8.11 us (3%)
  other arithmetic  3.61 us (1%)
    reduce_scatter x1, waiting for transfers between devices, on_device(): lax.psum_scatter(slot_term(broadcast_up, hidden, slots_per_worker * lax.a...  98 us
    reduce_scatter x1, waiting for transfers between devices, on_device(): lax.psum_scatter(slot_term(broadcast_down, output_gradient, slots_per_wor...  71.4 us
    psum x1, blocking collectives, on_device(): up_incoming = lax.psum(up_portion, 'tensor').astype(jnp.bfloat16)  30.2 us
    all_to_all x1, waiting for transfers between devices, launch_node(): jax.lax.all_to_all(latest, which_axis, 0, 0)  29.2 us
    all_gather x1, waiting for transfers between devices, on_device(): shard_portion = lax.all_gather(adapter_down, 'dp', axis=0, tiled=True)  20.8 us
    dot_general x2, matrix products, selected_rows(): lax.dot_general(value_entries, flattened_rows, (((1,), (1,)), ((), ())),...  13.3 us
    all_to_all x1, starting transfers between devices, launch_node(): jax.lax.all_to_all(latest, which_axis, 0, 0)  7.81 us
    dot_general x2, matrix products, slot_term(): lax.dot_general(broadcast_portion, value_entries, (((0,), (0,)), ((), ())...  7.15 us
  transfers between devices with their start and end apart: 4, of which 4 were waited for; matrix products, arithmetic and copies ran while one was open for 9% of the time, Pallas kernels for 0%

profile of v1, /device:TPU:2, one launch (start us, length us, event | category | flops | bytes accessed | tf_op | source)
XLA Modules:
  0.0 316.1 jit_solution(6398795008330522139)
XLA Ops:
  7.2 0.0 copy-start
  7.2 0.0 all-gather.2.cloned.1.call-start
  7.2 0.7 all-gather.2.cloned.1.call-update
  7.9 0.9 copy.18
  8.8 3.2 %stack.2 = bf16[32,2,16,1024]{3,1,2,0:T(2,128)(2,1)} broadcast(bf16[2,16,1024]{2,0,1:T(2,128)(2,1)S(1)} %copy.18), dimensions={1,2,3} | broadcast | bytes 2162688 | tf_op jit(solution)/shard_map/stack | solution.py:11
  12.0 0.0 copy-start.2
  12.0 0.0 copy-start.4
  12.0 0.0 copy-start.3
  12.0 7.8 %all-to-all-start = ((bf16[32,2,16,1024]{3,1,2,0:T(2,128)(2,1)}), bf16[32,2,16,1024]{3,1,2,0:T(2,128)(2,1)}, u32[]{:S(2)}, u32[]{:S(2)}) async-start(bf16[32,2,16,1024]{3,1,2,0:T(2,128)(2,1)} %stack.2), calls=%async_computation | async-start | bytes 4194304 | tf_op jit(solution)/shard_map/all_to_all | solution.py:12
  19.8 0.0 reduce-scatter.5.cloned.1.call-start
  19.9 0.0 copy-done.2
  19.9 0.0 copy-done.4
  19.9 0.0 copy-done.3
  20.0 0.1 select_reduce_fusion
  20.1 29.2 %all-to-all-done = bf16[32,2,16,1024]{3,1,2,0:T(2,128)(2,1)} async-done(((bf16[32,2,16,1024]{3,1,2,0:T(2,128)(2,1)}), bf16[32,2,16,1024]{3,1,2,0:T(2,128)(2,1)}, u32[]{:S(2)}, u32[]{:S(2)}) %all-to-all-start) | async-done | bytes 2097184 | tf_op jit(solution)/shard_map/all_to_all | solution.py:12
  49.3 4.8 %copy.19 = bf16[32,2,16,1024]{3,1,0,2:T(2,128)(2,1)} copy(bf16[32,2,16,1024]{3,1,2,0:T(2,128)(2,1)} %all-to-all-done) | data formatting | bytes 4194304 | tf_op jit(solution)/shard_map/all_to_all | solution.py:12
  54.1 0.0 copy-start.1
  54.1 4.2 %dot_general.25 = bf16[64,16,1024]{2,0,1:T(8,128)(2,1)} reshape(bf16[32,2,16,1024]{3,1,0,2:T(2,128)(2,1)} %copy.19) | data formatting | bytes 4194304 | tf_op jit(solution)/shard_map/dot_general | solution.py:22
  58.4 0.0 copy-done.1
  58.4 2.3 fusion.11
  60.7 20.8 %all-gather.2.cloned.1.call-done = bf16[64,16,3584]{2,1,0:T(8,128)(2,1)} async-done(((bf16[2,16,3584]{2,1,0:T(8,128)(2,1)}), bf16[64,16,3584]{2,1,0:T(8,128)(2,1)}) %all-gather.2.cloned.1.call-update) | async-done | bytes 7340048 | tf_op jit(solution)/shard_map/all_gather | solution.py:49
  81.5 0.0 copy-done
  81.5 11.0 %fusion.12 = f32[256,16]{0,1:T(8,128)S(1)} fusion(bf16[64,16,3584]{2,1,0:T(8,128)(2,1)} %all-gather.2.cloned.1.call-done, bf16[256,3584]{1,0:T(8,128)(2,1)S(1)} %copy-done, f32[256,64]{0,1:T(8,128)S(1)} %get-tuple-element.6), kind=kOutput, calls=%fused_computation.12 | convolution fusion | flops 1879568384 | bytes 9256960 | tf_op jit(solution)/shard_map/dot_general | solution.py:22
  92.4 30.2 %all-reduce = (bf16[256,16]{0,1:T(8,128)(2,1)S(1)}, bf16[256,16]{0,1:T(8,128)(2,1)S(1)}) all-reduce(f32[256,16]{0,1:T(8,128)S(1)} %fusion.11, f32[256,16]{0,1:T(8,128)S(1)} %fusion.12), channel_id=1, replica_groups=mesh['dp'=32,'tensor'=8] {'tensor'}, use_global_device_ids=true, to_apply=%region_2.3 | all-reduce | flops 8192 | bytes 49152 | tf_op jit(solution)/shard_map/psum | solution.py:47
  122.7 2.0 convolution_convert_fusion.1
  124.7 0.0 reduce-scatter.5.cloned.1.call-update
  124.8 0.2 reduce-scatter.3.cloned.1.call-start
  125.0 5.1 %convolution_convert_fusion = bf16[64,16,3584]{2,1,0:T(8,128)(2,1)} fusion(bf16[256,3584]{1,0:T(8,128)(2,1)S(1)} %copy-done, bf16[256,16]{0,1:T(8,128)(2,1)S(1)} %get-tuple-element.3, bf16[256,64]{0,1:T(8,128)(2,1)S(1)} %get-tuple-element.5), kind=kOutput, calls=%fused_computation | convolution fusion | flops 1882980352 | bytes 9216000 | tf_op jit(solution)/shard_map/dot_general | solution.py:66
  130.1 0.0 reduce-scatter.3.cloned.1.call-update
  130.1 0.1 select_reduce_fusion.1
  130.2 0.1 dynamic_slice.3
  130.3 6.5 %fusion.3 = bf16[256,3584]{1,0:T(8,128)(2,1)} fusion(bf16[64,16,3584]{2,1,0:T(8,128)(2,1)} %all-gather.2.cloned.1.call-done, bf16[256,16]{0,1:T(8,128)(2,1)S(1)} %get-tuple-element.3, bf16[256,64]{0,1:T(8,128)(2,1)S(1)} %get-tuple-element.5), kind=kOutput, calls=%fused_computation.5 | convolution fusion | flops 1881145344 | bytes 9216000 | tf_op jit(solution)/shard_map/dot_general | solution.py:55
  136.8 71.4 %reduce-scatter.5.cloned.1.call-done = bf16[2,16,1024]{2,1,0:T(8,128)(2,1)} async-done(((bf16[64,16,1024]{2,1,0:T(8,128)(2,1)}), bf16[2,16,1024]{2,1,0:T(8,128)(2,1)}) %reduce-scatter.5.cloned.1.call-update) | async-done | bytes 65552 | tf_op jit(solution)/shard_map/reduce_scatter | solution.py:82
  208.2 1.6 convert_multiply_fusion.1
  209.8 98.0 %reduce-scatter.3.cloned.1.call-done = bf16[2,16,3584]{2,1,0:T(8,128)(2,1)} async-done(((bf16[64,16,3584]{2,1,0:T(8,128)(2,1)}), bf16[2,16,3584]{2,1,0:T(8,128)(2,1)}) %reduce-scatter.3.cloned.1.call-update) | async-done | bytes 229392 | tf_op jit(solution)/shard_map/reduce_scatter | solution.py:74
  307.8 1.8 convert_multiply_fusion
  (4 shorter events, 0.0 us)
Async XLA Ops:
  7.2 74.3 %copy-start = (bf16[256,3584]{1,0:T(8,128)(2,1)S(1)}, bf16[256,3584]{1,0:T(8,128)(2,1)}, u32[]{:S(2)}) copy-start(bf16[256,3584]{1,0:T(8,128)(2,1)} %param.8) | copy-start | bytes 5505028
  7.2 74.3 %all-gather.2.cloned.1.call-start = ((), (), s32[]{:S(2)}) async-start(), calls=%async_computation.3 | async-start | bytes 7569408 | tf_op jit(solution)/shard_map/all_gather | solution.py:49
  12.0 7.9 %copy-start.2 = (s32[64]{0:T(128)S(1)}, s32[64]{0:T(128)}, u32[]{:S(2)}) copy-start(s32[64]{0:T(128)} %param.12) | copy-start | bytes 772
  12.0 7.9 %copy-start.4 = (s32[64]{0:T(128)S(1)}, s32[64]{0:T(128)}, u32[]{:S(2)}) copy-start(s32[64]{0:T(128)} %param.11) | copy-start | bytes 772
  12.0 7.9 %copy-start.3 = (s32[64]{0:T(128)S(1)}, s32[64]{0:T(128)}, u32[]{:S(2)}) copy-start(s32[64]{0:T(128)} %param.13) | copy-start | bytes 772
  12.0 37.2 %all-to-all-start = ((bf16[32,2,16,1024]{3,1,2,0:T(2,128)(2,1)}), bf16[32,2,16,1024]{3,1,2,0:T(2,128)(2,1)}, u32[]{:S(2)}, u32[]{:S(2)}) async-start(bf16[32,2,16,1024]{3,1,2,0:T(2,128)(2,1)} %stack.2), calls=%async_computation | async-start | bytes 4194304 | tf_op jit(solution)/shard_map/all_to_all | solution.py:12
  19.8 188.4 %reduce-scatter.5.cloned.1.call-start = ((), (), s32[]{:S(2)}) async-start(), calls=%async_computation.5 | async-start | bytes 2162688 | tf_op jit(solution)/shard_map/reduce_scatter | solution.py:82
  54.1 4.2 %copy-start.1 = (bf16[256,1024]{1,0:T(8,128)(2,1)S(1)}, bf16[256,1024]{1,0:T(8,128)(2,1)}, u32[]{:S(2)}) copy-start(bf16[256,1024]{1,0:T(8,128)(2,1)} %param.7) | copy-start | bytes 1572868
  124.8 183.1 %reduce-scatter.3.cloned.1.call-start = ((), (), s32[]{:S(2)}) async-start(), calls=%async_computation.4 | async-start | bytes 7569408 | tf_op jit(solution)/shard_map/reduce_scatter | solution.py:74
Sparse Core Ops, SparseCore 0:
  10.5 70.9 all-gather.1
  124.9 83.2 reduce-scatter.4
  212.3 95.4 reduce-scatter.2
